TPU v7x, 128 devices: a whole 4x4x4 slice. The times are simulated.
128 devices in a mesh: cls: 8 (over y, core), mem: 16 (over z, x).
Axes of the slice: x: 4, y: 4, z: 4, core: 2. Of those that a mesh axis runs over, the one named last changes fastest.
Arguments:
- images: bfloat16 [3072, 65536], P(('cls', 'mem')), may hold values from -6 to 6
- owner_group: int32 [3072, 1], P(('cls', 'mem')), may hold values from 0 to 7; in each aligned block of 24 rows (0 to 23, 24 to 47, ...) at most 6 rows name the same one
- bin_in_group: int32 [3072], P(('cls', 'mem')), may hold values from 0 to 7
- defocus: bfloat16 [3072], P(('cls', 'mem')), may hold values from 0.5 to 2
- projections: bfloat16 [64, 65536], P('cls'), may hold values from -6 to 6
- sketch_weight: bfloat16 [64, 48], replicated, may hold values from -0.875 to 0.875
Outputs:
- basis: bfloat16 [8, 64, 65536], P('cls', None, 'mem')
Inputs may be any that keep to these rules, and one draw needn't show every extreme that they name: `owner_group`: in the particles of one device no class group is named more than 6 times, and 6 is reached on some device.
All inputs are finite; a program needn't handle non-finite values.
Results may differ from a plain program's by a relative error of at most 0.012.
The roundings to bfloat16 on the way count: a program that leaves them out, or rounds other values in their place, can miss the bound.
Values may be sent and summed in bfloat16 or wider, within the bound.
A program may use at most 128 MiB of HBM per device.

v0:
```python
import math
import jax
import jax.numpy as jnp
from jax import lax
from jax.sharding import PartitionSpec as P

SIDE = 256
CAP = 6
HI = lax.Precision.HIGHEST


def wave_slice(first, width):
    position = first + jnp.arange(width, dtype=jnp.int32)
    column = position % SIDE
    row_idx = position // SIDE
    fx = jnp.where(column < SIDE // 2, column, column - SIDE).astype(jnp.float32) / SIDE
    fy = jnp.where(row_idx < SIDE // 2, row_idx, row_idx - SIDE).astype(jnp.float32) / SIDE
    return 160.0 * (fx * fx + fy * fy)


def bmm(a, b):
    return jnp.einsum("nij,njk->nik", a, b, precision=HI)


def coefficients(gram, pixels):
    total = jnp.trace(gram, axis1=1, axis2=2)[:, None, None] + 1e-06
    scaled = gram / total
    ident = jnp.eye(gram.shape[1], dtype=jnp.float32)[None]
    first = 1.5 * ident - 0.5 * scaled
    later = bmm(bmm(first, scaled), first)
    second = 1.5 * ident - 0.5 * later
    return bmm(second, first) * jnp.sqrt(pixels / total)


def tree(gram, n_mem, rank, pixels):
    blocks = n_mem
    k = gram.reshape(n_mem, rank, n_mem, rank)
    chain = None
    while True:
        diag = jnp.stack([k[i, :, i, :] for i in range(blocks)])
        c = coefficients(diag, pixels)
        if chain is None:
            chain = c[:, :, None, :]
        else:
            chain = jnp.einsum("nij,njmk->nimk", c, chain, precision=HI)
        if blocks == 1:
            return chain.reshape(rank, n_mem * rank)
        k = jnp.einsum("aij,ajbk->aibk", c, k, precision=HI)
        k = jnp.einsum("aibk,blk->aibl", k, c, precision=HI)
        half = blocks // 2
        k = k.reshape(half, 2, rank, half, 2, rank).sum(axis=(1, 4))
        chain = (
            chain.reshape(half, 2, rank, -1, rank)
            .transpose(0, 2, 1, 3, 4)
            .reshape(half, rank, -1, rank)
        )
        blocks = half


def body(images, owner_group, bin_in_group, defocus, projections, sketch_weight):
    n_cls = lax.axis_size("cls")
    n_mem = lax.axis_size("mem")
    pixels = images.shape[1]
    width = pixels // n_mem
    member = lax.axis_index("mem")
    cls = lax.axis_index("cls")
    p_dev = images.shape[0]
    bins_here = projections.shape[0]
    rank_k = sketch_weight.shape[0]
    owners = owner_group[:, 0]
    onehot = (owners[:, None] == jnp.arange(n_cls, dtype=jnp.int32)[None, :]).astype(jnp.int32)
    before = jnp.cumsum(onehot, axis=0) - onehot
    rank = jnp.sum(onehot * before, axis=1)
    target = owners * CAP + rank
    meta = jnp.stack(
        [target.astype(jnp.float32), defocus.astype(jnp.float32), bin_in_group.astype(jnp.float32)]
    )
    meta = lax.all_gather(meta, ("cls", "mem"), tiled=False).reshape(n_cls, n_mem, 3, p_dev)
    rows = lax.all_to_all(images, "mem", split_axis=1, concat_axis=0, tiled=True)
    rows = rows.reshape(n_mem, p_dev, width)
    mine = lax.dynamic_index_in_dim(meta, cls, 0, keepdims=False)[:, 0]
    select = jnp.arange(n_cls * CAP, dtype=jnp.float32)[None, :, None] == mine[:, None, :]
    sent = jnp.einsum(
        "mti,mip->mtp", select.astype(jnp.bfloat16), rows, preferred_element_type=jnp.float32
    ).astype(jnp.bfloat16)
    sent = (
        sent.reshape(n_mem, n_cls, CAP, width)
        .transpose(1, 0, 2, 3)
        .reshape(n_cls * n_mem * CAP, width)
    )
    got = lax.all_to_all(sent, "cls", split_axis=0, concat_axis=0, tiled=True)
    slot = (cls * CAP + jnp.arange(CAP, dtype=jnp.int32)).astype(jnp.float32)
    pick = (slot[None, None, :, None] == meta[:, :, None, 0, :]).astype(jnp.float32)
    focus = jnp.sum(pick * meta[:, :, None, 1, :], axis=-1).reshape(-1)
    local_bin = jnp.sum(pick * meta[:, :, None, 2, :], axis=-1)
    valid = jnp.sum(pick, axis=-1)
    bins = jnp.arange(bins_here, dtype=jnp.float32)
    table = jnp.where((local_bin[..., None] == bins) & (valid[..., None] > 0.5), 1.0, 0.0)
    table = table.reshape(-1, bins_here).astype(jnp.bfloat16)
    proj = lax.dynamic_slice_in_dim(projections, member * width, width, 1)
    chosen = jnp.dot(table, proj, preferred_element_type=jnp.float32)
    chi = focus[:, None] * wave_slice(member * width, width)[None, :]
    ctf = -math.sqrt(1.01) * jnp.sin(chi + math.atan(0.1))
    residual = (got.astype(jnp.float32) - ctf * chosen).astype(jnp.bfloat16)
    residual = (
        residual.reshape(n_cls, n_mem, CAP, width)
        .transpose(1, 0, 2, 3)
        .reshape(n_mem, n_cls * CAP, width)
    )
    sketch = jnp.einsum(
        "ks,msp->mkp", sketch_weight, residual, preferred_element_type=jnp.float32
    ).astype(jnp.bfloat16)
    sketch = sketch.reshape(n_mem * rank_k, width)
    gram = jnp.einsum("ap,bp->ab", sketch, sketch, preferred_element_type=jnp.float32)
    gram = lax.psum(gram, "mem")
    coef = tree(gram, n_mem, rank_k, float(pixels)).astype(jnp.bfloat16)
    result = jnp.dot(coef, sketch, preferred_element_type=jnp.float32).astype(jnp.bfloat16)
    return result[None]


def solution(mesh):
    in_specs = (
        P(("cls", "mem"), None),
        P(("cls", "mem"), None),
        P(("cls", "mem")),
        P(("cls", "mem")),
        P("cls", None),
        P(),
    )
    out_specs = P("cls", None, "mem")
    return jax.shard_map(body, mesh=mesh, in_specs=in_specs, out_specs=out_specs, check_vma=False)
```

profile of v0, /device:TPU:1, one launch (start us, length us, event | category | flops | bytes accessed | tf_op | source)
XLA Modules:
  0.0 546.3 jit_solution(17044176956349966713)
XLA Ops:
  6.5 4.0 copy.191
  10.6 8.5 %all-to-all-start = ((bf16[24,16,4096]{2,0,1:T(8,128)(2,1)}), bf16[24,16,4096]{2,0,1:T(8,128)(2,1)}, u32[]{:S(2)}, u32[]{:S(2)}) async-start(bf16[24,16,4096]{2,0,1:T(8,128)(2,1)} %bitcast.266), calls=%async_computation | async-start | bytes 6291456 | tf_op jit(solution)/shard_map/all_to_all | solution.py:79
  19.4 96.3 %all-gather.1 = f32[128,3,24]{2,1,0:T(4,128)S(1)} all-gather(f32[1,3,24]{2,1,0:T(4,128)S(1)} %maximum_bitcast_fusion), channel_id=2, replica_groups=mesh['cls'=8,'mem'=16] {'cls','mem'}, dimensions={0}, use_global_device_ids=true | all-gather | bytes 37152 | tf_op jit(solution)/shard_map/all_gather | solution.py:78
  115.8 3.8 convolution_convert_fusion.1
  119.6 3.4 copy.115
  123.1 3.4 copy.116
  126.5 6.3 %copy.117 = bf16[8,96,4096]{2,1,0:T(8,128)(2,1)} copy(bf16[8,96,4096]{2,0,1:T(8,128)(2,1)S(1)} %bitcast.264) | data formatting | bytes 12582912 | tf_op jit(solution)/shard_map/all_to_all | solution.py:91
  132.8 5.8 %all-to-all-start.1 = ((bf16[8,96,4096]{2,1,0:T(8,128)(2,1)}), bf16[8,96,4096]{2,1,0:T(8,128)(2,1)}, u32[]{:S(2)}, u32[]{:S(2)}) async-start(bf16[8,96,4096]{2,1,0:T(8,128)(2,1)} %copy.117), calls=%async_computation.1 | async-start | bytes 12582912 | tf_op jit(solution)/shard_map/all_to_all | solution.py:91
  138.8 0.4 fusion.22
  140.1 69.9 %all-to-all-done.1 = bf16[8,96,4096]{2,1,0:T(8,128)(2,1)} async-done(((bf16[8,96,4096]{2,1,0:T(8,128)(2,1)}), bf16[8,96,4096]{2,1,0:T(8,128)(2,1)}, u32[]{:S(2)}, u32[]{:S(2)}) %all-to-all-start.1) | async-done | bytes 6291488 | tf_op jit(solution)/shard_map/all_to_all | solution.py:91
  210.0 47.5 %fusion = bf16[768,4096]{1,0:T(8,128)(2,1)} fusion(bf16[768,4096]{1,0:T(8,128)(2,1)} %bitcast.88, f32[4096]{0:T(1024)S(1)} %fusion.85, f32[768]{0:T(1024)S(1)} %mul.219, f32[768]{0:T(1024)S(1)} %eq.134, pred[768]{0:T(1024)(128)(4,1)S(1)} %gt.16, bf16[8,65536]{1,0:T(8,128)(2,1)S(1)} %copy-done, s32[]{:T(128)S(6)} %select_n.80), kind=kOutput, calls=%fused_computation.1 | convolution fusion | flops 72376320 | bytes 12674052 | tf_op jit(solution)/shard_map/dot_general | solution.py:101
  257.5 10.1 %reshape.271 = bf16[8,16,6,4096]{3,2,1,0:T(8,128)(2,1)} reshape(bf16[768,4096]{1,0:T(8,128)(2,1)} %fusion) | data formatting | bytes 12582912 | tf_op jit(solution)/shard_map/reshape | solution.py:106
  267.7 7.0 %copy.125 = bf16[16,8,6,4096]{3,0,2,1:T(8,128)(2,1)S(1)} copy(bf16[16,8,6,4096]{3,2,0,1:T(8,128)(2,1)} %bitcast.261) | data formatting | bytes 12582912 | tf_op jit(solution)/shard_map/transpose | solution.py:107
  274.6 5.7 %convolution_convert_fusion = bf16[16,4096,64]{1,2,0:T(8,128)(2,1)S(1)} fusion(bf16[16,48,4096]{2,0,1:T(8,128)(2,1)S(1)} %bitcast.265, bf16[64,48]{0,1:T(8,128)(2,1)S(1)} %copy-done.4), kind=kOutput, calls=%fused_computation.4 | convolution fusion | flops 406847488 | bytes 14686208 | tf_op jit(solution)/shard_map/ks,msp->mkp/dot_general | solution.py:110
  280.3 3.2 copy-done.2
  283.5 10.8 %fusion.140 = f32[1024,1024]{1,0:T(8,128)} fusion(bf16[1024,4096]{1,0:T(8,128)(2,1)S(1)} %bitcast.259), kind=kOutput, calls=%fused_computation.242 | convolution fusion | flops 8589934592 | bytes 12582912 | tf_op jit(solution)/shard_map/ap,bp->ab/dot_general | solution.py:114
  294.3 7.3 %reshape.274 = f32[16,64,16,64]{3,2,1,0:T(8,128)} reshape(f32[1024,1024]{1,0:T(8,128)} %fusion.140) | data formatting | bytes 8388608 | tf_op jit(solution)/shard_map/reshape | solution.py:37
  301.6 9.2 %copy.127 = f32[16,64,16,64]{3,1,2,0:T(8,128)} copy(f32[16,64,16,64]{3,2,1,0:T(8,128)} %reshape.274) | data formatting | bytes 8388608 | tf_op jit(solution)/shard_map/reshape | solution.py:37
  310.9 139.2 %all-reduce.2.cloned.1.call-done = f32[16,64,16,64]{3,1,2,0:T(8,128)} async-done(((f32[16,64,16,64]{3,1,2,0:T(8,128)}), f32[16,64,16,64]{3,1,2,0:T(8,128)}) %all-reduce.2.cloned.1.call-update) | async-done | bytes 4194320 | tf_op jit(solution)/shard_map/psum | solution.py:115
  450.1 0.9 constant_dynamic-update-slice_fusion.15
  451.0 0.9 constant_dynamic-update-slice_fusion.14
  451.9 1.1 constant_dynamic-update-slice_fusion.13
  453.0 0.8 constant_dynamic-update-slice_fusion.12
  453.7 0.8 constant_dynamic-update-slice_fusion.11
  454.5 0.8 constant_dynamic-update-slice_fusion.10
  455.2 0.8 constant_dynamic-update-slice_fusion.9
  456.0 0.8 constant_dynamic-update-slice_fusion.8
  456.8 0.8 constant_dynamic-update-slice_fusion.7
  457.5 0.8 constant_dynamic-update-slice_fusion.6
  458.3 0.8 constant_dynamic-update-slice_fusion.5
  459.0 0.8 constant_dynamic-update-slice_fusion.4
  459.8 0.8 constant_dynamic-update-slice_fusion.3
  460.6 0.8 constant_dynamic-update-slice_fusion.2
  461.3 0.8 constant_dynamic-update-slice_fusion.1
  462.1 0.8 constant_dynamic-update-slice_fusion
  463.1 0.8 fusion.19
  463.9 0.7 fusion.6
  464.6 0.7 convolution_multiply_fusion
  465.3 8.7 %fusion.1 = f32[16,64,16,64]{3,1,0,2:T(8,128)S(1)} fusion(f32[16,64,16,64]{3,1,2,0:T(8,128)S(1)} %copy-done.3, f32[16,64,64]{2,1,0:T(8,128)S(1)} %convolution_multiply_fusion), kind=kOutput, calls=%fused_computation.2 | convolution fusion | flops 805306368 | bytes 8650752 | tf_op jit(solution)/shard_map/aij,ajbk->aibk/dot_general | solution.py:48
  474.0 26.4 %fusion.16 = f32[16,64,16,64]{3,1,2,0:T(8,128)} fusion(f32[16,64,16,64]{3,1,0,2:T(8,128)S(1)} %fusion.1, f32[16,64,64]{2,1,0:T(8,128)S(1)} %convolution_multiply_fusion), kind=kOutput, calls=%fused_computation.36 | convolution fusion | flops 805306368 | bytes 8650752 | tf_op jit(solution)/shard_map/aibk,blk->aibl/dot_general | solution.py:49
  500.4 4.6 reduce_sum.131
  506.0 0.5 fusion.30
  506.5 0.4 fusion.7
  506.9 0.4 convolution_multiply_fusion.2
  507.4 6.1 %fusion.28 = f32[8,64,8,64]{3,1,0,2:T(8,128)S(1)} fusion(f32[8,64,8,64]{1,3,0,2:T(8,128)S(1)} %reduce_sum.131, f32[8,64,64]{2,1,0:T(8,128)S(1)} %convolution_multiply_fusion.2), kind=kOutput, calls=%fused_computation.53 | convolution fusion | flops 201326592 | bytes 2228224 | tf_op jit(solution)/shard_map/aij,ajbk->aibk/dot_general | solution.py:48
  513.5 1.4 fusion.24
  514.8 6.0 %fusion.26 = f32[8,64,8,64]{3,1,2,0:T(8,128)S(1)} fusion(f32[8,64,8,64]{3,1,0,2:T(8,128)S(1)} %fusion.28, f32[8,64,64]{2,1,0:T(8,128)S(1)} %convolution_multiply_fusion.2), kind=kOutput, calls=%fused_computation.51 | convolution fusion | flops 201326592 | bytes 2228224 | tf_op jit(solution)/shard_map/aibk,blk->aibl/dot_general | solution.py:49
  520.9 0.3 reduce_sum.133
  521.6 0.4 fusion.48
  522.0 0.3 fusion.8
  522.3 0.3 convolution_multiply_fusion.4
  522.7 1.6 fusion.46
  524.3 1.9 fusion.14
  526.2 1.6 fusion.42
  528.2 0.3 fusion.60
  528.5 0.3 fusion.9
  528.7 0.3 convolution_multiply_fusion.6
  529.0 0.5 fusion.44
  529.5 0.6 fusion.12
  530.1 0.3 copy.192
  530.6 0.3 fusion.10
  531.0 0.6 fusion.69
  532.9 0.4 convolution_convert_fusion.3
  533.3 5.7 %fusion.4 = bf16[1,64,4096]{2,1,0:T(8,128)(2,1)} fusion(bf16[64,1024]{1,0:T(8,128)(2,1)S(1)} %convolution_convert_fusion.3, bf16[1024,4096]{1,0:T(8,128)(2,1)} %bitcast.260), kind=kOutput, calls=%fused_computation.8 | convolution fusion | flops 537133056 | bytes 9043968 | tf_op jit(solution)/shard_map/dot_general | solution.py:117
  (79 shorter events, 4.1 us)
Async XLA Ops:
  6.5 203.5 %copy-start = (bf16[8,65536]{1,0:T(8,128)(2,1)S(1)}, bf16[8,65536]{1,0:T(8,128)(2,1)}, u32[]{:S(2)}) copy-start(bf16[8,65536]{1,0:T(8,128)(2,1)} %param.10) | copy-start | bytes 3145732
  6.5 12.5 %copy-start.5 = (s32[24,1]{0,1:T(1,128)S(1)}, s32[24,1]{0,1:T(1,128)}, u32[]{:S(2)}) copy-start(s32[24,1]{0,1:T(1,128)} %param.7) | copy-start | bytes 292
  6.5 12.8 %copy-start.6 = (s32[24]{0:T(128)S(1)}, s32[24]{0:T(128)}, u32[]{:S(2)}) copy-start(s32[24]{0:T(128)} %param.8) | copy-start | bytes 292
  6.5 12.9 %copy-start.7 = (bf16[24]{0:T(256)(128)(2,1)S(1)}, bf16[24]{0:T(256)(128)(2,1)}, u32[]{:S(2)}) copy-start(bf16[24]{0:T(256)(128)(2,1)} %param.9) | copy-start | bytes 148
  10.6 105.2 %all-to-all-start = ((bf16[24,16,4096]{2,0,1:T(8,128)(2,1)}), bf16[24,16,4096]{2,0,1:T(8,128)(2,1)}, u32[]{:S(2)}, u32[]{:S(2)}) async-start(bf16[24,16,4096]{2,0,1:T(8,128)(2,1)} %bitcast.266), calls=%async_computation | async-start | bytes 6291456 | tf_op jit(solution)/shard_map/all_to_all | solution.py:79
  132.8 77.2 %all-to-all-start.1 = ((bf16[8,96,4096]{2,1,0:T(8,128)(2,1)}), bf16[8,96,4096]{2,1,0:T(8,128)(2,1)}, u32[]{:S(2)}, u32[]{:S(2)}) async-start(bf16[8,96,4096]{2,1,0:T(8,128)(2,1)} %copy.117), calls=%async_computation.1 | async-start | bytes 12582912 | tf_op jit(solution)/shard_map/all_to_all | solution.py:91
  138.6 311.4 %all-reduce.2.cloned.1.call-start = ((), (), s32[]{:S(2)}) async-start(), calls=%async_computation.2 | async-start | bytes 16777216 | tf_op jit(solution)/shard_map/psum | solution.py:115
  267.6 7.0 %copy-start.4 = (bf16[64,48]{0,1:T(8,128)(2,1)S(1)}, bf16[64,48]{0,1:T(8,128)(2,1)}, u32[]{:S(2)}) copy-start(bf16[64,48]{0,1:T(8,128)(2,1)} %param.11) | copy-start | bytes 18436
  280.3 3.2 copy-start.2
  450.1 15.3 %copy-start.3 = (f32[16,64,16,64]{3,1,2,0:T(8,128)S(1)}, f32[16,64,16,64]{3,1,2,0:T(8,128)}, u32[]{:S(2)}) copy-start(f32[16,64,16,64]{3,1,2,0:T(8,128)} %all-reduce.2.cloned.1.call-done) | copy-start | bytes 12582916
  530.4 8.6 %copy-start.1 = (bf16[8,65536]{1,0:T(8,128)(2,1)S(1)}, bf16[8,65536]{1,0:T(8,128)(2,1)}, u32[]{:S(2)}) copy-start(bf16[8,65536]{1,0:T(8,128)(2,1)} %param.10) | copy-start | bytes 3145732
Sparse Core Ops, SparseCore 0:
  310.9 139.0 all-reduce.1
where the time goes:
time: 557 us; the launch traced here: 546 us
  waiting for transfers between devices  209 us (38%)
  matrix products  135 us (24%)
  blocking collectives  96.3 us (17%)
  local copies, waits for them, and re-layouts  69.5 us (12%)
  between operations  15.1 us (3%)
  starting transfers between devices  14.3 us (3%)
  other arithmetic  7.06 us (1%)
    psum x1, waiting for transfers between devices, body(): gram = lax.psum(gram, 'mem')  139 us
    all_gather x1, blocking collectives, body(): lax.all_gather(meta, ('cls', 'mem'), tiled=False)  96.3 us
    all_to_all x1, waiting for transfers between devices, body(): got = lax.all_to_all(sent, 'cls', split_axis=0, concat_axis=0, tiled=True)  69.9 us
    dot_general x1, matrix products, body(): chosen = jnp.dot(table, proj, preferred_element_type=jnp.float32)  47.5 us
    dot_general x4, matrix products, tree(): k = jnp.einsum('aibk,blk->aibl', k, c, precision=HI)  34.3 us
    dot_general x4, matrix products, tree(): k = jnp.einsum('aij,ajbk->aibk', c, k, precision=HI)  16.8 us
    reshape x2, local copies, waits for them, and re-layouts, tree(): k = gram.reshape(n_mem, rank, n_mem, rank)  16.5 us
    unnamed x52, local copies, waits for them, and re-layouts  16.4 us
  transfers between devices with their start and end apart: 3, of which 2 were waited for; matrix products, arithmetic and copies ran while one was open for 0% of the time, Pallas kernels for 0%

commit v1 on v0

--- a/solution.py
+++ b/solution.py
@@ -112,7 +112,9 @@
     ).astype(jnp.bfloat16)
     sketch = sketch.reshape(n_mem * rank_k, width)
     gram = jnp.einsum("ap,bp->ab", sketch, sketch, preferred_element_type=jnp.float32)
-    gram = lax.psum(gram, "mem")
+    gram = gram
+    for hop in (1, 2, 4, 8):
+        gram = gram + lax.ppermute(gram, "mem", [(dev, dev ^ hop) for dev in range(16)])
     coef = tree(gram, n_mem, rank_k, float(pixels)).astype(jnp.bfloat16)
     result = jnp.dot(coef, sketch, preferred_element_type=jnp.float32).astype(jnp.bfloat16)
     return result[None]

time: 557 us -> 765 us (1.37)
  waiting for transfers between devices: 209 us -> 428 us
  between operations: 15.1 us -> 1.62 us
  local copies, waits for them, and re-layouts: 69.5 us -> 59.6 us
    ppermute x0 -> x4, waiting for transfers between devices: none -> 358 us  [body(): lax.ppermute(gram, 'mem', [(dev, dev ^ hop) for dev in range(16)])]
    psum x1 -> x0, waiting for transfers between devices: 139 us -> none  [body(): gram = lax.psum(gram, 'mem')]
    unnamed x52 -> x54, local copies, waits for them, and re-layouts: 16.4 us -> 1.28 us
    all_to_all x1, local copies, waits for them, and re-layouts: 6.28 us -> 18.5 us  [body(): got = lax.all_to_all(sent, 'cls', split_axis=0, concat_axis=0, tiled=True)]
    reshape x2 -> x1, local copies, waits for them, and re-layouts: 16.5 us -> 7.42 us  [tree(): k = gram.reshape(n_mem, rank, n_mem, rank)]
  transfers between devices with their start and end apart: 3 -> 6, of which waited for: 2 -> 5; matrix products, arithmetic and copies ran while one was open for 0% -> 0% of each run, Pallas kernels for 0% -> 0%
where the time goes in v1:
time: 765 us; the launch traced here: 752 us
  waiting for transfers between devices  428 us (56%)
  matrix products  134 us (18%)
  blocking collectives  96.3 us (13%)
  local copies, waits for them, and re-layouts  59.6 us (8%)
  starting transfers between devices  19 us (2%)
  other arithmetic  13.6 us (2%)
    ppermute x4, waiting for transfers between devices, body(): lax.ppermute(gram, 'mem', [(dev, dev ^ hop) for dev in range(16)])  358 us
    all_gather x1, blocking collectives, body(): lax.all_gather(meta, ('cls', 'mem'), tiled=False)  96.3 us
    all_to_all x1, waiting for transfers between devices, body(): got = lax.all_to_all(sent, 'cls', split_axis=0, concat_axis=0, tiled=True)  69.9 us
    dot_general x1, matrix products, body(): chosen = jnp.dot(table, proj, preferred_element_type=jnp.float32)  47.5 us
    dot_general x4, matrix products, tree(): k = jnp.einsum('aibk,blk->aibl', k, c, precision=HI)  34.5 us
    dot_general x4, matrix products, tree(): k = jnp.einsum('aij,ajbk->aibk', c, k, precision=HI)  18.9 us
    all_to_all x1, local copies, waits for them, and re-layouts, body(): got = lax.all_to_all(sent, 'cls', split_axis=0, concat_axis=0, tiled=True)  18.5 us
  transfers between devices with their start and end apart: 6, of which 5 were waited for; matrix products, arithmetic and copies ran while one was open for 0% of the time, Pallas kernels for 0%

profile of v1, /device:TPU:1, one launch (start us, length us, event | category | flops | bytes accessed | tf_op | source)
XLA Modules:
  0.0 752.3 jit_solution(8823286163376510310)
XLA Ops:
  0.0 4.0 copy.297
  4.1 8.5 %all-to-all-start = ((bf16[24,16,4096]{2,0,1:T(8,128)(2,1)}), bf16[24,16,4096]{2,0,1:T(8,128)(2,1)}, u32[]{:S(2)}, u32[]{:S(2)}) async-start(bf16[24,16,4096]{2,0,1:T(8,128)(2,1)} %bitcast.250), calls=%async_computation | async-start | bytes 6291456 | tf_op jit(solution)/shard_map/all_to_all | solution.py:79
  12.7 0.2 select_reduce_fusion.4
  12.9 96.3 %all-gather.1 = f32[128,3,24]{2,1,0:T(4,128)S(1)} all-gather(f32[1,3,24]{2,1,0:T(4,128)S(1)} %maximum_bitcast_fusion), channel_id=2, replica_groups=mesh['cls'=8,'mem'=16] {'cls','mem'}, dimensions={0}, use_global_device_ids=true | all-gather | bytes 37152 | tf_op jit(solution)/shard_map/all_gather | solution.py:78
  109.3 3.8 convolution_convert_fusion.1
  113.1 3.4 copy.190
  116.5 3.4 copy.191
  120.0 18.5 %copy.192 = bf16[8,96,4096]{2,1,0:T(8,128)(2,1)} copy(bf16[8,96,4096]{2,0,1:T(8,128)(2,1)S(1)} %bitcast.248) | data formatting | bytes 12582912 | tf_op jit(solution)/shard_map/all_to_all | solution.py:91
  138.4 5.8 all-to-all-start.1
  144.4 0.4 fusion.22
  145.7 69.9 %all-to-all-done.1 = bf16[8,96,4096]{2,1,0:T(8,128)(2,1)} async-done(((bf16[8,96,4096]{2,1,0:T(8,128)(2,1)}), bf16[8,96,4096]{2,1,0:T(8,128)(2,1)}, u32[]{:S(2)}, u32[]{:S(2)}) %all-to-all-start.1) | async-done | bytes 6291488 | tf_op jit(solution)/shard_map/all_to_all | solution.py:91
  215.7 47.5 %fusion = bf16[768,4096]{1,0:T(8,128)(2,1)} fusion(bf16[768,4096]{1,0:T(8,128)(2,1)} %bitcast.88, f32[4096]{0:T(1024)S(1)} %fusion.85, f32[768]{0:T(1024)S(1)} %mul.219, f32[768]{0:T(1024)S(1)} %eq.134, pred[768]{0:T(1024)(128)(4,1)S(1)} %gt.16, bf16[8,65536]{1,0:T(8,128)(2,1)S(1)} %copy-done, s32[]{:T(128)S(6)} %select_n.80), kind=kOutput, calls=%fused_computation.1 | convolution fusion | flops 72376320 | bytes 12674052 | tf_op jit(solution)/shard_map/dot_general | solution.py:101
  263.2 10.1 %reshape.271 = bf16[8,16,6,4096]{3,2,1,0:T(8,128)(2,1)} reshape(bf16[768,4096]{1,0:T(8,128)(2,1)} %fusion) | data formatting | bytes 12582912 | tf_op jit(solution)/shard_map/reshape | solution.py:106
  273.3 7.0 copy.200
  280.3 5.7 convolution_convert_fusion
  286.0 9.3 %fusion.141 = f32[1024,1024]{1,0:T(8,128)S(1)} fusion(bf16[1024,4096]{1,0:T(8,128)(2,1)S(1)} %bitcast.243), kind=kOutput, calls=%fused_computation.227 | convolution fusion | flops 8589934592 | bytes 12582912 | tf_op jit(solution)/shard_map/ap,bp->ab/dot_general | solution.py:114
  295.4 91.2 %collective-permute-done = f32[1024,1024]{1,0:T(8,128)S(1)} collective-permute-done((f32[1024,1024]{1,0:T(8,128)S(1)}, f32[1024,1024]{1,0:T(8,128)S(1)}, u32[]{:S(2)}, u32[]{:S(2)}) %collective-permute-start) | collective-permute-done | bytes 4194336 | tf_op jit(solution)/shard_map/ppermute | solution.py:117
  386.5 0.9 add.148
  387.5 1.3 collective-permute-start.1
  388.7 90.6 %collective-permute-done.1 = f32[1024,1024]{1,0:T(8,128)S(1)} collective-permute-done((f32[1024,1024]{1,0:T(8,128)S(1)}, f32[1024,1024]{1,0:T(8,128)S(1)}, u32[]{:S(2)}, u32[]{:S(2)}) %collective-permute-start.1) | collective-permute-done | bytes 4194336 | tf_op jit(solution)/shard_map/ppermute | solution.py:117
  479.4 1.4 add.149
  480.7 0.8 collective-permute-start.2
  481.5 88.7 %collective-permute-done.2 = f32[1024,1024]{1,0:T(8,128)S(1)} collective-permute-done((f32[1024,1024]{1,0:T(8,128)S(1)}, f32[1024,1024]{1,0:T(8,128)S(1)}, u32[]{:S(2)}, u32[]{:S(2)}) %collective-permute-start.2) | collective-permute-done | bytes 4194336 | tf_op jit(solution)/shard_map/ppermute | solution.py:117
  570.2 1.4 add.150
  571.5 2.6 collective-permute-start.3
  574.1 87.4 %collective-permute-done.3 = f32[1024,1024]{1,0:T(8,128)S(1)} collective-permute-done((f32[1024,1024]{1,0:T(8,128)S(1)}, f32[1024,1024]{1,0:T(8,128)S(1)}, u32[]{:S(2)}, u32[]{:S(2)}) %collective-permute-start.3) | collective-permute-done | bytes 4194336 | tf_op jit(solution)/shard_map/ppermute | solution.py:117
  661.6 2.9 add.151
  664.4 7.4 reshape.274
  671.8 2.8 fusion.136
  674.9 0.2 select_reduce_fusion
  675.1 0.8 fusion.19
  675.9 0.7 fusion.6
  676.6 0.7 convolution_multiply_fusion
  677.4 10.7 %fusion.1 = f32[16,64,16,64]{3,1,0,2:T(8,128)S(1)} fusion(f32[16,64,16,64]{3,2,1,0:T(8,128)S(1)} %copy-done.2, f32[16,64,64]{2,1,0:T(8,128)S(1)} %convolution_multiply_fusion), kind=kOutput, calls=%fused_computation.2 | convolution fusion | flops 805306368 | bytes 8650752 | tf_op jit(solution)/shard_map/aij,ajbk->aibk/dot_general | solution.py:48
  688.1 26.5 %fusion.16 = f32[16,64,16,64]{3,1,2,0:T(8,128)} fusion(f32[16,64,16,64]{3,1,0,2:T(8,128)S(1)} %fusion.1, f32[16,64,64]{2,1,0:T(8,128)S(1)} %convolution_multiply_fusion), kind=kOutput, calls=%fused_computation.36 | convolution fusion | flops 805306368 | bytes 8650752 | tf_op jit(solution)/shard_map/aibk,blk->aibl/dot_general | solution.py:49
  714.7 4.6 reduce_sum.131
  720.1 0.2 select_reduce_fusion.1
  720.3 0.5 fusion.30
  720.8 0.4 fusion.7
  721.2 0.4 convolution_multiply_fusion.2
  721.7 6.1 fusion.28
  727.7 1.4 fusion.24
  729.1 6.0 fusion.26
  735.2 0.3 reduce_sum.133
  735.9 0.4 fusion.48
  736.3 0.3 fusion.8
  736.6 0.3 convolution_multiply_fusion.4
  737.0 1.6 fusion.46
  738.6 0.7 fusion.14
  739.3 1.6 fusion.42
  741.3 0.3 fusion.60
  741.6 0.3 fusion.9
  741.9 0.3 convolution_multiply_fusion.6
  742.1 0.5 fusion.44
  742.6 0.6 fusion.12
  743.2 0.3 copy.298
  743.5 0.2 dot_general.131
  743.7 0.3 fusion.10
  744.1 0.6 fusion.69
  745.4 0.2 fusion.76
  745.6 0.2 fusion.11
  745.8 0.2 convolution_multiply_fusion.8
  746.0 0.4 convolution_convert_fusion.3
  746.4 5.7 fusion.4
  (90 shorter events, 3.1 us)
Async XLA Ops:
  0.0 215.7 %copy-start = (bf16[8,65536]{1,0:T(8,128)(2,1)S(1)}, bf16[8,65536]{1,0:T(8,128)(2,1)}, u32[]{:S(2)}) copy-start(bf16[8,65536]{1,0:T(8,128)(2,1)} %param.10) | copy-start | bytes 3145732
  0.0 12.5 %copy-start.6 = (s32[24,1]{0,1:T(1,128)S(1)}, s32[24,1]{0,1:T(1,128)}, u32[]{:S(2)}) copy-start(s32[24,1]{0,1:T(1,128)} %param.7) | copy-start | bytes 292
  0.0 12.8 %copy-start.7 = (s32[24]{0:T(128)S(1)}, s32[24]{0:T(128)}, u32[]{:S(2)}) copy-start(s32[24]{0:T(128)} %param.8) | copy-start | bytes 292
  0.0 12.9 %copy-start.8 = (bf16[24]{0:T(256)(128)(2,1)S(1)}, bf16[24]{0:T(256)(128)(2,1)}, u32[]{:S(2)}) copy-start(bf16[24]{0:T(256)(128)(2,1)} %param.9) | copy-start | bytes 148
  4.1 105.2 %all-to-all-start = ((bf16[24,16,4096]{2,0,1:T(8,128)(2,1)}), bf16[24,16,4096]{2,0,1:T(8,128)(2,1)}, u32[]{:S(2)}, u32[]{:S(2)}) async-start(bf16[24,16,4096]{2,0,1:T(8,128)(2,1)} %bitcast.250), calls=%async_computation | async-start | bytes 6291456 | tf_op jit(solution)/shard_map/all_to_all | solution.py:79
  138.4 77.2 %all-to-all-start.1 = ((bf16[8,96,4096]{2,1,0:T(8,128)(2,1)}), bf16[8,96,4096]{2,1,0:T(8,128)(2,1)}, u32[]{:S(2)}, u32[]{:S(2)}) async-start(bf16[8,96,4096]{2,1,0:T(8,128)(2,1)} %copy.192), calls=%async_computation.1 | async-start | bytes 12582912 | tf_op jit(solution)/shard_map/all_to_all | solution.py:91
  273.3 7.0 copy-start.5
  286.0 9.3 %copy-start.3 = (bf16[16,4096,64]{1,2,0:T(8,128)(2,1)}, bf16[16,4096,64]{1,2,0:T(8,128)(2,1)S(1)}, u32[]{:S(2)}) copy-start(bf16[16,4096,64]{1,2,0:T(8,128)(2,1)S(1)} %convolution_convert_fusion) | copy-start | bytes 25165828
  295.3 91.3 %collective-permute-start = (f32[1024,1024]{1,0:T(8,128)S(1)}, f32[1024,1024]{1,0:T(8,128)S(1)}, u32[]{:S(2)}, u32[]{:S(2)}) collective-permute-start(f32[1024,1024]{1,0:T(8,128)S(1)} %fusion.141), channel_id=1, source_target_pairs={{0,1},{1,0},{2,3},{3,2},{4,5},{5,4},{6,7},{7,6},{8,9},{9,8},{10,11... | collective-permute-start | bytes 12582920 | tf_op jit(solution)/shard_map/ppermute | solution.py:117
  387.5 91.9 %collective-permute-start.1 = (f32[1024,1024]{1,0:T(8,128)S(1)}, f32[1024,1024]{1,0:T(8,128)S(1)}, u32[]{:S(2)}, u32[]{:S(2)}) collective-permute-start(f32[1024,1024]{1,0:T(8,128)S(1)} %add.148), channel_id=1, source_target_pairs={{0,2},{1,3},{2,0},{3,1},{4,6},{5,7},{6,4},{7,5},{8,10},{9,11},{10,... | collective-permute-start | bytes 12582920 | tf_op jit(solution)/shard_map/ppermute | solution.py:117
  480.7 89.4 %collective-permute-start.2 = (f32[1024,1024]{1,0:T(8,128)S(1)}, f32[1024,1024]{1,0:T(8,128)S(1)}, u32[]{:S(2)}, u32[]{:S(2)}) collective-permute-start(f32[1024,1024]{1,0:T(8,128)S(1)} %add.149), channel_id=1, source_target_pairs={{0,4},{1,5},{2,6},{3,7},{4,0},{5,1},{6,2},{7,3},{8,12},{9,13},{10,... | collective-permute-start | bytes 12582920 | tf_op jit(solution)/shard_map/ppermute | solution.py:117
  571.5 90.0 %collective-permute-start.3 = (f32[1024,1024]{1,0:T(8,128)S(1)}, f32[1024,1024]{1,0:T(8,128)S(1)}, u32[]{:S(2)}, u32[]{:S(2)}) collective-permute-start(f32[1024,1024]{1,0:T(8,128)S(1)} %add.150), channel_id=1, source_target_pairs={{0,8},{1,9},{2,10},{3,11},{4,12},{5,13},{6,14},{7,15},{8,0},{9,1},... | collective-permute-start | bytes 12582920 | tf_op jit(solution)/shard_map/ppermute | solution.py:117
  671.8 5.5 copy-start.2
  735.2 3.4 copy-start.4
  746.0 6.1 copy-start.1
